TPU v7x, 512 devices: a whole 4x4x16 slice. The times are simulated.
512 devices in a mesh: dom: 64 (over z, x_lo, core), bin: 8 (over y, x_hi).
Axes of the slice: x: 4 (x_hi: 2, x_lo: 2; x = x_hi * 2 + x_lo), y: 4, z: 16, core: 2. Of those that a mesh axis runs over, the one named last changes fastest.
Arguments:
- dust_rho: float32 [128, 65536], P('bin', 'dom'), may hold values from 0.25 to 4
- dust_vel: float32 [2, 128, 65536], P(None, 'bin', 'dom'), may hold values from -4 to 4
- gas_rho: float32 [65536], P('dom'), may hold values from 50 to 500
- gas_vel: float32 [2, 65536], P(None, 'dom'), may hold values from -4 to 4
- normals: float32 [2, 8, 65536], P(None, None, 'dom'), may hold values from -0.24 to 0.24
- inv_volume: float32 [65536], P('dom'), may hold values from 0.75 to 3
- coag_rate: float32 [65536], P('dom'), may hold values from 0.03 to 0.3
- drag_coef: float32 [128], P('bin'), as said below
- neighbours: int32 [8, 65536], P(None, 'dom'), may hold values from -1 to 1535, as said below
- send_cells: int32 [64, 4, 128], P('dom'), may hold values from -1 to 1023, as said below
- kernel: bfloat16 [128, 128], replicated, may hold values from 0.001953125 to 0.0703125, as said below
- redistrib: bfloat16 [128, 128], replicated, may hold values from -0.5 to 0.5
Outputs:
- dust_rho_out: float32 [128, 65536], P('bin', 'dom')
- dust_vel_out: float32 [2, 128, 65536], P(None, 'bin', 'dom')
- gas_vel_out: float32 [2, 65536], P(None, 'dom')
Inputs may be any that keep to these rules, and one draw needn't show every extreme that they name: Row send_cells[d, j] lists distinct cells of domain d, then -1 in the remaining slots; every row has 32 or more cells, and all rows of some domain are full. `neighbours`: an entry is -1, another local cell of the same domain, or 1024 + j * 128 + p for a ghost slot p that the sending domain fills; slot 0 of every cell is valid. `drag_coef`: Positive. `kernel`: positive and symmetric.
All inputs are finite; a program needn't handle non-finite values.
Results may differ from a plain program's by a relative error of at most 0.0048.
Values may be sent and summed in bfloat16 or wider, within the bound.
A program may use at most 64 MiB of HBM per device.

v0:
```python
import jax
import jax.numpy as jnp
from jax import lax
from jax.sharding import PartitionSpec as P

OFFSETS = (1, -1, 2, -2)


def from_behind(value, axis, steps):
    count = lax.axis_size(axis)
    pairs = [(source, (source + steps) % count) for source in range(count)]
    return lax.ppermute(value, axis, pairs)


def minmod(first, second):
    return 0.5 * (jnp.sign(first) + jnp.sign(second)) * jnp.minimum(jnp.abs(first), jnp.abs(second))


def advect(state, extended_rows, faces, face_normals, inv_vol):
    density = state[0]
    vel_x = state[1]
    vel_y = state[2]
    bin_rows = density.shape[0]
    cell_count = density.shape[1]
    face_count = faces.shape[0]
    valid_all = faces >= 0
    safe_all = jnp.maximum(faces, 0).reshape(face_count * cell_count)
    picked = jnp.take(extended_rows, safe_all, axis=0)
    picked = picked.reshape(face_count, cell_count, 3, bin_rows)
    picked = jnp.transpose(picked, (0, 2, 3, 1))
    total_mean = jnp.zeros_like(density)
    valid_count = jnp.zeros(density.shape[1:], jnp.float32)
    for face in range(face_count):
        valid = valid_all[face]
        total_mean = total_mean + jnp.where(valid, picked[face, 0], 0.0)
        valid_count = valid_count + valid.astype(jnp.float32)
    neighbour_mean = total_mean / valid_count
    flux_total = jnp.zeros_like(density)
    for face in range(face_count):
        valid = valid_all[face]
        other = picked[face, 0]
        speed = 0.5 * (
            (vel_x + picked[face, 1]) * face_normals[0, face]
            + (vel_y + picked[face, 2]) * face_normals[1, face]
        )
        limited = minmod(other - density, density - neighbour_mean)
        flux = jnp.maximum(speed, 0.0) * (density + 0.5 * limited) + jnp.minimum(speed, 0.0) * (
            other - 0.5 * limited
        )
        flux_total = flux_total + jnp.where(valid, flux, 0.0)
    return density - inv_vol * flux_total


def body(
    dust_rho,
    dust_vel,
    gas_rho,
    gas_vel,
    normals,
    inv_volume,
    coag_rate,
    drag_coef,
    neighbours,
    send_cells,
    kernel,
    redistrib,
):
    own_rows = dust_rho.shape[0]
    cell_count = dust_rho.shape[1]
    coupling = drag_coef[:, None] * gas_rho[None, :]
    share = coupling / (1.0 + coupling)
    weight = dust_rho / gas_rho[None, :] * share
    partial_sums = jnp.stack(
        [
            jnp.sum(weight, axis=0),
            jnp.sum(weight * dust_vel[0], axis=0),
            jnp.sum(weight * dust_vel[1], axis=0),
        ]
    )
    totals = lax.psum(partial_sums, "bin")
    gas_new = (gas_vel + totals[1:]) / (1.0 + totals[0])
    dust_vel_new = (dust_vel + coupling[None] * gas_new[:, None, :]) / (1.0 + coupling[None])
    state = jnp.concatenate([dust_rho[None], dust_vel_new], axis=0)
    state_rows = jnp.transpose(state.reshape(3 * own_rows, cell_count))
    blocks = [state_rows]
    for direction, offset in enumerate(OFFSETS):
        index = send_cells[0, direction]
        chosen = (
            jnp.take(state_rows, jnp.maximum(index, 0), axis=0)
            * (index >= 0).astype(jnp.float32)[:, None]
        )
        blocks.append(from_behind(chosen, "dom", offset))
    extended_rows = jnp.concatenate(blocks, axis=0)
    moved = advect(state, extended_rows, neighbours, normals, inv_volume)
    rounded = moved.astype(jnp.bfloat16)
    first_bin = lax.axis_index("bin") * own_rows
    kernel_rows = lax.dynamic_slice_in_dim(kernel, first_bin, own_rows, 0)
    columns = kernel_rows
    collide = jnp.dot(
        columns,
        lax.all_gather(rounded, "bin", axis=0, tiled=True),
        preferred_element_type=jnp.float32,
    )
    loss = (coag_rate[None, :] * rounded.astype(jnp.float32) * collide).astype(jnp.bfloat16)
    redis_rows = lax.dynamic_slice_in_dim(redistrib, first_bin, own_rows, 0)
    columns = redis_rows
    gain = jnp.dot(
        columns, lax.all_gather(loss, "bin", axis=0, tiled=True), preferred_element_type=jnp.float32
    )
    dust_rho_out = moved - loss.astype(jnp.float32) + gain
    return (dust_rho_out, dust_vel_new, gas_new)


def solution(mesh):
    placed = (
        P("bin", "dom"),
        P(None, "bin", "dom"),
        P("dom"),
        P(None, "dom"),
        P(None, None, "dom"),
        P("dom"),
        P("dom"),
        P("bin"),
        P(None, "dom"),
        P("dom", None, None),
        P(),
        P(),
    )
    return jax.shard_map(
        body,
        mesh=mesh,
        in_specs=placed,
        out_specs=(P("bin", "dom"), P(None, "bin", "dom"), P(None, "dom")),
        check_vma=False,
    )
```

profile of v0, /device:TPU:98, one launch (start us, length us, event | category | flops | bytes accessed | tf_op | source)
XLA Modules:
  0.0 177.4 jit_solution(4021776785599090148)
XLA Ops:
  0.6 0.0 copy-start
  0.6 0.8 compare_and_fusion
  1.5 0.8 fusion.65
  2.3 1.0 broadcast_multiply_fusion
  3.3 0.9 fusion.51
  4.2 41.3 %psum.7 = f32[3,1024]{1,0:T(4,128)S(1)} all-reduce(f32[3,1024]{1,0:T(4,128)S(1)} %pad_maximum_fusion.1), channel_id=1, replica_groups=mesh['dom'=64,'bin'=8] {'bin'}, use_global_device_ids=true, to_apply=%region_3.0 | all-reduce | flops 3072 | bytes 24576 | tf_op jit(solution)/shard_map/psum | solution.py:80
  45.5 0.7 fusion.52
  46.2 0.0 copy-start.5
  46.2 0.9 add_divide_fusion
  47.1 0.0 copy-start.1
  47.2 0.9 pad_maximum_fusion
  48.1 0.2 copy.28
  48.3 0.6 gather_fusion.1
  48.9 0.1 select_multiply_fusion.3
  49.0 1.9 %collective-permute-start = (f32[128,48]{1,0:T(8,128)S(1)}, f32[128,48]{1,0:T(8,128)S(1)}, u32[]{:S(2)}, u32[]{:S(2)}) collective-permute-start(f32[128,48]{1,0:T(8,128)S(1)} %select_multiply_fusion.3), channel_id=1, source_target_pairs={{0,8},{8,16},{16,24},{24,32},{32,40},{40,48},{48,56},{56,64},{64,7... | collective-permute-start | bytes 73736 | tf_op jit(solution)/shard_map/ppermute | solution.py:12
  51.0 0.0 copy-start.3
  51.0 0.6 gather_fusion.2
  51.6 0.0 copy-start.4
  51.6 0.1 select_multiply_fusion.2
  51.7 3.6 %collective-permute-start.1 = (f32[128,48]{1,0:T(8,128)S(1)}, f32[128,48]{1,0:T(8,128)S(1)}, u32[]{:S(2)}, u32[]{:S(2)}) collective-permute-start(f32[128,48]{1,0:T(8,128)S(1)} %select_multiply_fusion.2), channel_id=1, source_target_pairs={{0,504},{8,0},{16,8},{24,16},{32,24},{40,32},{48,40},{56,48},{64,5... | collective-permute-start | bytes 73736 | tf_op jit(solution)/shard_map/ppermute | solution.py:12
  55.4 0.6 gather_fusion.3
  56.1 0.0 copy-done.5
  56.1 0.1 select_multiply_fusion.1
  56.2 8.0 %collective-permute-start.2 = (f32[128,48]{1,0:T(8,128)S(1)}, f32[128,48]{1,0:T(8,128)S(1)}, u32[]{:S(2)}, u32[]{:S(2)}) collective-permute-start(f32[128,48]{1,0:T(8,128)S(1)} %select_multiply_fusion.1), channel_id=1, source_target_pairs={{0,16},{8,24},{16,32},{24,40},{32,48},{40,56},{48,64},{56,72},{64,... | collective-permute-start | bytes 73736 | tf_op jit(solution)/shard_map/ppermute | solution.py:12
  64.2 0.6 gather_fusion.4
  64.8 0.1 select_multiply_fusion
  65.0 1.9 %collective-permute-start.3 = (f32[128,48]{1,0:T(8,128)S(1)}, f32[128,48]{1,0:T(8,128)S(1)}, u32[]{:S(2)}, u32[]{:S(2)}) collective-permute-start(f32[128,48]{1,0:T(8,128)S(1)} %select_multiply_fusion), channel_id=1, source_target_pairs={{0,496},{8,504},{16,0},{24,8},{32,16},{40,24},{48,32},{56,40},{64,... | collective-permute-start | bytes 73736 | tf_op jit(solution)/shard_map/ppermute | solution.py:12
  66.9 0.0 copy-done.3
  67.1 0.0 copy-done.4
  67.2 0.1 slice_reduce_fusion.7
  67.3 0.0 collective-permute-done
  67.3 0.0 collective-permute-done.1
  67.3 0.0 collective-permute-done.2
  67.4 5.9 %collective-permute-done.3 = f32[128,48]{1,0:T(8,128)S(1)} collective-permute-done((f32[128,48]{1,0:T(8,128)S(1)}, f32[128,48]{1,0:T(8,128)S(1)}, u32[]{:S(2)}, u32[]{:S(2)}) %collective-permute-start.3) | collective-permute-done | bytes 24608 | tf_op jit(solution)/shard_map/ppermute | solution.py:12
  73.2 27.7 %gather_fusion = f32[8192,48]{1,0:T(8,128)} fusion(f32[1536,48]{1,0:T(8,128)S(1)} %constant_dynamic-update-slice_fusion, s32[8192]{0:T(1024)S(1)} %broadcast_clamp_fusion), kind=kCustom, calls=%fused_computation.4 | custom fusion | bytes 3178496 | tf_op jit(solution)/shard_map/jit(_take)/gather | solution.py:28
  100.9 2.8 %copy.29 = f32[8192,48]{0,1:T(8,128)S(1)} copy(f32[8192,48]{1,0:T(8,128)} %gather_fusion) | data formatting | bytes 3145728 | tf_op jit(solution)/shard_map/jit(_take)/gather | solution.py:28
  103.7 0.9 copy.32
  104.6 0.0 copy-start.2
  104.7 0.0 copy-start.6
  104.7 1.0 fusion
  105.7 0.0 copy-start.7
  105.7 0.0 copy-done.1
  105.7 0.0 copy-done.2
  105.7 0.0 copy-done.6
  105.7 0.6 fusion.68
  106.3 34.8 %all_gather.6 = bf16[128,1024]{1,0:T(8,128)(2,1)S(1)} all-gather(bf16[16,1024]{1,0:T(8,128)(2,1)S(1)} %get-tuple-element.15), channel_id=1, replica_groups=mesh['dom'=64,'bin'=8] {'bin'}, dimensions={0}, use_global_device_ids=true | all-gather | bytes 294912 | tf_op jit(solution)/shard_map/all_gather | solution.py:101
  141.1 0.0 copy-done
  141.1 0.0 copy-done.7
  141.1 0.2 fusion.1
  141.3 34.7 %all_gather.7 = bf16[128,1024]{1,0:T(8,128)(2,1)S(1)} all-gather(bf16[16,1024]{1,0:T(8,128)(2,1)S(1)} %fusion.1), channel_id=1, replica_groups=mesh['dom'=64,'bin'=8] {'bin'}, dimensions={0}, use_global_device_ids=true | all-gather | bytes 294912 | tf_op jit(solution)/shard_map/all_gather | solution.py:108
  175.9 1.5 convolution_add_fusion
  (18 shorter events, 0.3 us)
Async XLA Ops:
  0.6 140.5 %copy-start = (bf16[128,128]{1,0:T(8,128)(2,1)S(1)}, bf16[128,128]{1,0:T(8,128)(2,1)}, u32[]{:S(2)}) copy-start(bf16[128,128]{1,0:T(8,128)(2,1)} %param.24) | copy-start | bytes 98308
  46.2 9.9 %copy-start.5 = (f32[2,1024]{1,0:T(2,128)}, f32[2,1024]{1,0:T(2,128)S(1)}, u32[]{:S(2)}) copy-start(f32[2,1024]{1,0:T(2,128)S(1)} %fusion.52) | copy-start | bytes 24580
  47.1 58.6 %copy-start.1 = (f32[2,16,1024]{2,1,0:T(8,128)}, f32[2,16,1024]{2,1,0:T(8,128)S(1)}, u32[]{:S(2)}) copy-start(f32[2,16,1024]{2,1,0:T(8,128)S(1)} %add_divide_fusion) | copy-start | bytes 393220
  49.0 18.3 %collective-permute-start = (f32[128,48]{1,0:T(8,128)S(1)}, f32[128,48]{1,0:T(8,128)S(1)}, u32[]{:S(2)}, u32[]{:S(2)}) collective-permute-start(f32[128,48]{1,0:T(8,128)S(1)} %select_multiply_fusion.3), channel_id=1, source_target_pairs={{0,8},{8,16},{16,24},{24,32},{32,40},{40,48},{48,56},{56,64},{64,7... | collective-permute-start | bytes 73736 | tf_op jit(solution)/shard_map/ppermute | solution.py:12
  51.0 16.0 %copy-start.3 = (s32[8,1024]{1,0:T(8,128)S(1)}, s32[8,1024]{1,0:T(8,128)}, u32[]{:S(2)}) copy-start(s32[8,1024]{1,0:T(8,128)} %param.22) | copy-start | bytes 98308
  51.6 15.4 %copy-start.4 = (f32[2,8,1024]{2,1,0:T(8,128)S(1)}, f32[2,8,1024]{2,1,0:T(8,128)}, u32[]{:S(2)}) copy-start(f32[2,8,1024]{2,1,0:T(8,128)} %param.18) | copy-start | bytes 196612
  51.7 15.6 %collective-permute-start.1 = (f32[128,48]{1,0:T(8,128)S(1)}, f32[128,48]{1,0:T(8,128)S(1)}, u32[]{:S(2)}, u32[]{:S(2)}) collective-permute-start(f32[128,48]{1,0:T(8,128)S(1)} %select_multiply_fusion.2), channel_id=1, source_target_pairs={{0,504},{8,0},{16,8},{24,16},{32,24},{40,32},{48,40},{56,48},{64,5... | collective-permute-start | bytes 73736 | tf_op jit(solution)/shard_map/ppermute | solution.py:12
  56.2 11.2 %collective-permute-start.2 = (f32[128,48]{1,0:T(8,128)S(1)}, f32[128,48]{1,0:T(8,128)S(1)}, u32[]{:S(2)}, u32[]{:S(2)}) collective-permute-start(f32[128,48]{1,0:T(8,128)S(1)} %select_multiply_fusion.1), channel_id=1, source_target_pairs={{0,16},{8,24},{16,32},{24,40},{32,48},{40,56},{48,64},{56,72},{64,... | collective-permute-start | bytes 73736 | tf_op jit(solution)/shard_map/ppermute | solution.py:12
  65.0 8.3 %collective-permute-start.3 = (f32[128,48]{1,0:T(8,128)S(1)}, f32[128,48]{1,0:T(8,128)S(1)}, u32[]{:S(2)}, u32[]{:S(2)}) collective-permute-start(f32[128,48]{1,0:T(8,128)S(1)} %select_multiply_fusion), channel_id=1, source_target_pairs={{0,496},{8,504},{16,0},{24,8},{32,16},{40,24},{48,32},{56,40},{64,... | collective-permute-start | bytes 73736 | tf_op jit(solution)/shard_map/ppermute | solution.py:12
  104.6 1.1 copy-start.2
  104.7 1.1 copy-start.6
  105.7 35.4 %copy-start.7 = (f32[1024]{0:T(1024)S(1)}, f32[1024]{0:T(1024)}, u32[]{:S(2)}) copy-start(f32[1024]{0:T(1024)} %param.20) | copy-start | bytes 12292
where the time goes:
time: 178 us; the launch traced here: 177 us
  blocking collectives  111 us (62%)
  local copies, waits for them, and re-layouts  34.5 us (19%)
  starting transfers between devices  15.5 us (9%)
  other arithmetic  8.26 us (5%)
  waiting for transfers between devices  5.86 us (3%)
    psum x1, blocking collectives, body(): totals = lax.psum(partial_sums, 'bin')  41.3 us
    all_gather x1, blocking collectives, body(): lax.all_gather(rounded, 'bin', axis=0, tiled=True)  34.8 us
    all_gather x1, blocking collectives, body(): lax.all_gather(loss, 'bin', axis=0, tiled=True)  34.7 us
    gather x2, local copies, waits for them, and re-layouts, advect(): picked = jnp.take(extended_rows, safe_all, axis=0)  30.5 us
    ppermute x4, starting transfers between devices, from_behind(): return lax.ppermute(value, axis, pairs)  15.5 us
    ppermute x4, waiting for transfers between devices, from_behind(): return lax.ppermute(value, axis, pairs)  5.86 us
  transfers between devices with their start and end apart: 4, of which 1 were waited for; matrix products, arithmetic and copies ran while one was open for 1% of the time, Pallas kernels for 0%

commit v1 on v0

--- a/solution.py
+++ b/solution.py
@@ -98,7 +98,9 @@
     columns = kernel_rows
     collide = jnp.dot(
         columns,
-        lax.all_gather(rounded, "bin", axis=0, tiled=True),
+        jnp.concatenate(
+            lax.all_to_all(jnp.stack([rounded] * lax.axis_size("bin")), "bin", 0, 0), axis=0
+        ),
         preferred_element_type=jnp.float32,
     )
     loss = (coag_rate[None, :] * rounded.astype(jnp.float32) * collide).astype(jnp.bfloat16)

time: 178 us -> 157 us (0.88)
  blocking collectives: 111 us -> 76.2 us
  waiting for transfers between devices: 5.86 us -> 14.6 us
  starting transfers between devices: 15.5 us -> 18.9 us
    all_gather x1 -> x0, blocking collectives: 34.8 us -> none  [body(): lax.all_gather(rounded, 'bin', axis=0, tiled=True)]
    all_to_all x0 -> x1, waiting for transfers between devices: none -> 8.72 us  [body(): lax.all_to_all(jnp.stack([rounded] * lax.axis_size('bin')), 'bin', 0, 0)]
    all_to_all x0 -> x1, starting transfers between devices: none -> 3.41 us  [body(): lax.all_to_all(jnp.stack([rounded] * lax.axis_size('bin')), 'bin', 0, 0)]
  transfers between devices with their start and end apart: 4 -> 5, of which waited for: 1 -> 2; matrix products, arithmetic and copies ran while one was open for 1% -> 2% of each run, Pallas kernels for 0% -> 0%
where the time goes in v1:
time: 157 us; the launch traced here: 156 us
  blocking collectives  76.2 us (49%)
  local copies, waits for them, and re-layouts  35.2 us (22%)
  starting transfers between devices  18.9 us (12%)
  waiting for transfers between devices  14.6 us (9%)
  other arithmetic  8.26 us (5%)
  matrix products  1.62 us (1%)
    psum x1, blocking collectives, body(): totals = lax.psum(partial_sums, 'bin')  41.3 us
    all_gather x1, blocking collectives, body(): lax.all_gather(loss, 'bin', axis=0, tiled=True)  35 us
    gather x2, local copies, waits for them, and re-layouts, advect(): picked = jnp.take(extended_rows, safe_all, axis=0)  30.5 us
    ppermute x4, starting transfers between devices, from_behind(): return lax.ppermute(value, axis, pairs)  15.5 us
    all_to_all x1, waiting for transfers between devices, body(): lax.all_to_all(jnp.stack([rounded] * lax.axis_size('bin')), 'bin', 0, 0)  8.72 us
    ppermute x4, waiting for transfers between devices, from_behind(): return lax.ppermute(value, axis, pairs)  5.86 us
    all_to_all x1, starting transfers between devices, body(): lax.all_to_all(jnp.stack([rounded] * lax.axis_size('bin')), 'bin', 0, 0)  3.41 us
  transfers between devices with their start and end apart: 5, of which 2 were waited for; matrix products, arithmetic and copies ran while one was open for 2% of the time, Pallas kernels for 0%

profile of v1, /device:TPU:98, one launch (start us, length us, event | category | flops | bytes accessed | tf_op | source)
XLA Modules:
  0.0 155.8 jit_solution(11632626445815436158)
XLA Ops:
  0.6 0.0 copy-start
  0.6 0.8 compare_and_fusion
  1.5 0.8 fusion.65
  2.3 1.0 broadcast_multiply_fusion
  3.3 0.9 fusion.51
  4.2 41.3 %psum.7 = f32[3,1024]{1,0:T(4,128)S(1)} all-reduce(f32[3,1024]{1,0:T(4,128)S(1)} %pad_maximum_fusion.1), channel_id=1, replica_groups=mesh['dom'=64,'bin'=8] {'bin'}, use_global_device_ids=true, to_apply=%region_3.0 | all-reduce | flops 3072 | bytes 24576 | tf_op jit(solution)/shard_map/psum | solution.py:80
  45.5 0.7 fusion.52
  46.2 0.0 copy-start.5
  46.2 0.9 add_divide_fusion
  47.1 0.0 copy-start.1
  47.2 0.9 pad_maximum_fusion
  48.1 0.2 copy.28
  48.3 0.6 gather_fusion.1
  48.9 0.1 select_multiply_fusion.3
  49.0 1.9 %collective-permute-start = (f32[128,48]{1,0:T(8,128)S(1)}, f32[128,48]{1,0:T(8,128)S(1)}, u32[]{:S(2)}, u32[]{:S(2)}) collective-permute-start(f32[128,48]{1,0:T(8,128)S(1)} %select_multiply_fusion.3), channel_id=1, source_target_pairs={{0,8},{8,16},{16,24},{24,32},{32,40},{40,48},{48,56},{56,64},{64,7... | collective-permute-start | bytes 73736 | tf_op jit(solution)/shard_map/ppermute | solution.py:12
  51.0 0.0 copy-start.3
  51.0 0.6 gather_fusion.2
  51.6 0.0 copy-start.4
  51.6 0.1 select_multiply_fusion.2
  51.7 3.6 %collective-permute-start.1 = (f32[128,48]{1,0:T(8,128)S(1)}, f32[128,48]{1,0:T(8,128)S(1)}, u32[]{:S(2)}, u32[]{:S(2)}) collective-permute-start(f32[128,48]{1,0:T(8,128)S(1)} %select_multiply_fusion.2), channel_id=1, source_target_pairs={{0,504},{8,0},{16,8},{24,16},{32,24},{40,32},{48,40},{56,48},{64,5... | collective-permute-start | bytes 73736 | tf_op jit(solution)/shard_map/ppermute | solution.py:12
  55.4 0.6 gather_fusion.3
  56.1 0.0 copy-done.5
  56.1 0.1 select_multiply_fusion.1
  56.2 8.0 %collective-permute-start.2 = (f32[128,48]{1,0:T(8,128)S(1)}, f32[128,48]{1,0:T(8,128)S(1)}, u32[]{:S(2)}, u32[]{:S(2)}) collective-permute-start(f32[128,48]{1,0:T(8,128)S(1)} %select_multiply_fusion.1), channel_id=1, source_target_pairs={{0,16},{8,24},{16,32},{24,40},{32,48},{40,56},{48,64},{56,72},{64,... | collective-permute-start | bytes 73736 | tf_op jit(solution)/shard_map/ppermute | solution.py:12
  64.2 0.6 gather_fusion.4
  64.8 0.1 select_multiply_fusion
  65.0 1.9 %collective-permute-start.3 = (f32[128,48]{1,0:T(8,128)S(1)}, f32[128,48]{1,0:T(8,128)S(1)}, u32[]{:S(2)}, u32[]{:S(2)}) collective-permute-start(f32[128,48]{1,0:T(8,128)S(1)} %select_multiply_fusion), channel_id=1, source_target_pairs={{0,496},{8,504},{16,0},{24,8},{32,16},{40,24},{48,32},{56,40},{64,... | collective-permute-start | bytes 73736 | tf_op jit(solution)/shard_map/ppermute | solution.py:12
  66.9 0.0 copy-done.3
  67.1 0.0 copy-done.4
  67.2 0.1 slice_reduce_fusion.7
  67.3 0.0 collective-permute-done
  67.3 0.0 collective-permute-done.1
  67.3 0.0 collective-permute-done.2
  67.4 5.9 %collective-permute-done.3 = f32[128,48]{1,0:T(8,128)S(1)} collective-permute-done((f32[128,48]{1,0:T(8,128)S(1)}, f32[128,48]{1,0:T(8,128)S(1)}, u32[]{:S(2)}, u32[]{:S(2)}) %collective-permute-start.3) | collective-permute-done | bytes 24608 | tf_op jit(solution)/shard_map/ppermute | solution.py:12
  73.2 27.7 %gather_fusion = f32[8192,48]{1,0:T(8,128)} fusion(f32[1536,48]{1,0:T(8,128)S(1)} %constant_dynamic-update-slice_fusion, s32[8192]{0:T(1024)S(1)} %broadcast_clamp_fusion), kind=kCustom, calls=%fused_computation.4 | custom fusion | bytes 3178496 | tf_op jit(solution)/shard_map/jit(_take)/gather | solution.py:28
  100.9 2.8 %copy.29 = f32[8192,48]{0,1:T(8,128)S(1)} copy(f32[8192,48]{1,0:T(8,128)} %gather_fusion) | data formatting | bytes 3145728 | tf_op jit(solution)/shard_map/jit(_take)/gather | solution.py:28
  103.7 0.9 copy.32
  104.6 0.0 copy-start.2
  104.7 0.0 copy-start.6
  104.7 1.0 fusion
  105.7 0.0 copy-start.7
  105.7 0.0 copy-done.1
  105.7 0.0 copy-done.2
  105.7 0.0 copy-done.6
  105.7 0.6 fusion.68
  106.3 0.7 stack.27
  107.1 3.4 %all-to-all-start = ((bf16[8,16,1024]{2,1,0:T(8,128)(2,1)}), bf16[8,16,1024]{2,1,0:T(8,128)(2,1)S(1)}, u32[]{:S(2)}, u32[]{:S(2)}) async-start(bf16[8,16,1024]{2,1,0:T(8,128)(2,1)} %stack.27), calls=%async_computation | async-start | bytes 524288 | tf_op jit(solution)/shard_map/all_to_all | solution.py:102
  110.5 8.7 %all-to-all-done = bf16[8,16,1024]{2,1,0:T(8,128)(2,1)S(1)} async-done(((bf16[8,16,1024]{2,1,0:T(8,128)(2,1)}), bf16[8,16,1024]{2,1,0:T(8,128)(2,1)S(1)}, u32[]{:S(2)}, u32[]{:S(2)}) %all-to-all-start) | async-done | bytes 262176 | tf_op jit(solution)/shard_map/all_to_all | solution.py:102
  119.2 0.0 copy-done
  119.2 0.0 copy-done.7
  119.2 0.2 fusion.1
  119.4 35.0 %all_gather.3 = bf16[128,1024]{1,0:T(8,128)(2,1)S(1)} all-gather(bf16[16,1024]{1,0:T(8,128)(2,1)S(1)} %fusion.1), channel_id=1, replica_groups=mesh['dom'=64,'bin'=8] {'bin'}, dimensions={0}, use_global_device_ids=true | all-gather | bytes 294912 | tf_op jit(solution)/shard_map/all_gather | solution.py:110
  154.3 1.5 convolution_add_fusion
  (18 shorter events, 0.3 us)
Async XLA Ops:
  0.6 118.6 %copy-start = (bf16[128,128]{1,0:T(8,128)(2,1)S(1)}, bf16[128,128]{1,0:T(8,128)(2,1)}, u32[]{:S(2)}) copy-start(bf16[128,128]{1,0:T(8,128)(2,1)} %param.24) | copy-start | bytes 98308
  46.2 9.9 %copy-start.5 = (f32[2,1024]{1,0:T(2,128)}, f32[2,1024]{1,0:T(2,128)S(1)}, u32[]{:S(2)}) copy-start(f32[2,1024]{1,0:T(2,128)S(1)} %fusion.52) | copy-start | bytes 24580
  47.1 58.6 %copy-start.1 = (f32[2,16,1024]{2,1,0:T(8,128)}, f32[2,16,1024]{2,1,0:T(8,128)S(1)}, u32[]{:S(2)}) copy-start(f32[2,16,1024]{2,1,0:T(8,128)S(1)} %add_divide_fusion) | copy-start | bytes 393220
  49.0 18.3 %collective-permute-start = (f32[128,48]{1,0:T(8,128)S(1)}, f32[128,48]{1,0:T(8,128)S(1)}, u32[]{:S(2)}, u32[]{:S(2)}) collective-permute-start(f32[128,48]{1,0:T(8,128)S(1)} %select_multiply_fusion.3), channel_id=1, source_target_pairs={{0,8},{8,16},{16,24},{24,32},{32,40},{40,48},{48,56},{56,64},{64,7... | collective-permute-start | bytes 73736 | tf_op jit(solution)/shard_map/ppermute | solution.py:12
  51.0 16.0 %copy-start.3 = (s32[8,1024]{1,0:T(8,128)S(1)}, s32[8,1024]{1,0:T(8,128)}, u32[]{:S(2)}) copy-start(s32[8,1024]{1,0:T(8,128)} %param.22) | copy-start | bytes 98308
  51.6 15.4 %copy-start.4 = (f32[2,8,1024]{2,1,0:T(8,128)S(1)}, f32[2,8,1024]{2,1,0:T(8,128)}, u32[]{:S(2)}) copy-start(f32[2,8,1024]{2,1,0:T(8,128)} %param.18) | copy-start | bytes 196612
  51.7 15.6 %collective-permute-start.1 = (f32[128,48]{1,0:T(8,128)S(1)}, f32[128,48]{1,0:T(8,128)S(1)}, u32[]{:S(2)}, u32[]{:S(2)}) collective-permute-start(f32[128,48]{1,0:T(8,128)S(1)} %select_multiply_fusion.2), channel_id=1, source_target_pairs={{0,504},{8,0},{16,8},{24,16},{32,24},{40,32},{48,40},{56,48},{64,5... | collective-permute-start | bytes 73736 | tf_op jit(solution)/shard_map/ppermute | solution.py:12
  56.2 11.2 %collective-permute-start.2 = (f32[128,48]{1,0:T(8,128)S(1)}, f32[128,48]{1,0:T(8,128)S(1)}, u32[]{:S(2)}, u32[]{:S(2)}) collective-permute-start(f32[128,48]{1,0:T(8,128)S(1)} %select_multiply_fusion.1), channel_id=1, source_target_pairs={{0,16},{8,24},{16,32},{24,40},{32,48},{40,56},{48,64},{56,72},{64,... | collective-permute-start | bytes 73736 | tf_op jit(solution)/shard_map/ppermute | solution.py:12
  65.0 8.3 %collective-permute-start.3 = (f32[128,48]{1,0:T(8,128)S(1)}, f32[128,48]{1,0:T(8,128)S(1)}, u32[]{:S(2)}, u32[]{:S(2)}) collective-permute-start(f32[128,48]{1,0:T(8,128)S(1)} %select_multiply_fusion), channel_id=1, source_target_pairs={{0,496},{8,504},{16,0},{24,8},{32,16},{40,24},{48,32},{56,40},{64,... | collective-permute-start | bytes 73736 | tf_op jit(solution)/shard_map/ppermute | solution.py:12
  104.6 1.1 copy-start.2
  104.7 1.1 copy-start.6
  105.7 13.5 %copy-start.7 = (f32[1024]{0:T(1024)S(1)}, f32[1024]{0:T(1024)}, u32[]{:S(2)}) copy-start(f32[1024]{0:T(1024)} %param.20) | copy-start | bytes 12292
  107.1 12.1 %all-to-all-start = ((bf16[8,16,1024]{2,1,0:T(8,128)(2,1)}), bf16[8,16,1024]{2,1,0:T(8,128)(2,1)S(1)}, u32[]{:S(2)}, u32[]{:S(2)}) async-start(bf16[8,16,1024]{2,1,0:T(8,128)(2,1)} %stack.27), calls=%async_computation | async-start | bytes 524288 | tf_op jit(solution)/shard_map/all_to_all | solution.py:102
